TPU v7x, 128 devices: a whole 4x4x4 slice. The times are simulated.
128 devices in a mesh: sensor: 16 (over y, z_lo, core), channel: 4 (over x), tm: 2 (over z_hi).
Axes of the slice: x: 4, y: 4, z: 4 (z_hi: 2, z_lo: 2; z = z_hi * 2 + z_lo), core: 2. Of those that a mesh axis runs over, the one named last changes fastest.
Arguments:
- tensor: float32 [12288, 128, 512], P('sensor', 'tm', 'channel'), may hold values from -6 to 6
- core: float32 [64, 64, 32], replicated, may hold values from -0.015625 to 0.015625
- sensor_factor: float32 [12288, 64], P('sensor'), may hold values from -6 to 6
- channel_factor: float32 [512, 64], P('channel'), may hold values from -6 to 6
- time_factor: float32 [128, 32], P('tm'), may hold values from -6 to 6
- neighbour_ids: int32 [96, 4], P('sensor'), may hold values from 0 to 95
- edge_weights: int32 [96, 4, 128, 128], P('sensor'), may hold values from 0 to 3
Outputs:
- core_grad: float32 [64, 64, 32], replicated
- sensor_grad: float32 [12288, 64], P(('sensor', 'channel', 'tm'))
- channel_grad: float32 [512, 64], P('channel')
- time_grad: float32 [128, 32], P('tm')
All inputs are finite; a program needn't handle non-finite values.
Results may differ from a plain program's by a relative error of at most 0.0001.
Values sent between devices are 32-bit elements; how exact they have to be, the bound alone decides.
A program may use at most 192 MiB of HBM per device.

v0:
```python
import math
import jax
import jax.numpy as jnp
from jax import lax
from jax.sharding import PartitionSpec as P

lap_weight = 1.0 / 512.0
highest = lax.Precision.HIGHEST


def pulled_rows(whole_factor, neighbour_ids, weights_float, block):
    whole = whole_factor.reshape(-1, block, whole_factor.shape[-1])
    neighbours = whole[neighbour_ids]
    return jnp.einsum("bnic,bncd->bid", weights_float, neighbours, precision=highest)


def on_device(
    tensor, core, sensor_factor, channel_factor, time_factor, neighbour_ids, edge_weights
):
    sensor_rows, time_rows, chan_rows = tensor.shape
    rank_one, rank_two, rank_three = core.shape
    n_sensor = lax.axis_size("sensor")
    n_channel = lax.axis_size("channel")
    n_time = lax.axis_size("tm")
    total_sensors = sensor_rows * n_sensor
    total_time = time_rows * n_time
    total_chan = chan_rows * n_channel
    core_time = jnp.einsum("rst,kt->rks", core, time_factor, precision=highest)
    core_both = jnp.einsum("rks,js->rkj", core_time, channel_factor, precision=highest)
    core_chan = jnp.einsum("rst,js->rtj", core, channel_factor, precision=highest)
    flat_core = core_both.reshape(rank_one, time_rows * chan_rows)
    residual = jnp.dot(sensor_factor, flat_core, precision=highest) - tensor.reshape(
        sensor_rows, time_rows * chan_rows
    )
    folded = jnp.dot(sensor_factor.T, residual, precision=highest)
    fit_part = jnp.dot(residual, flat_core.T, precision=highest) / math.sqrt(
        total_time * total_chan
    )
    folded3 = folded.reshape(rank_one, time_rows, chan_rows)
    inner = jnp.einsum("rkj,js->rks", folded3, channel_factor, precision=highest)
    core_part = jnp.einsum("rks,kt->rst", inner, time_factor, precision=highest) / math.sqrt(
        total_sensors * total_time * total_chan
    )
    chan_part = jnp.einsum("rkj,rks->js", folded3, core_time, precision=highest) / math.sqrt(
        total_sensors * total_time
    )
    time_part = jnp.einsum("rkj,rtj->kt", folded3, core_chan, precision=highest) / math.sqrt(
        total_sensors * total_chan
    )
    groups = n_channel * n_time
    share_index = lax.axis_index("channel") * n_time + lax.axis_index("tm")
    share = sensor_rows // groups
    block = edge_weights.shape[-1]
    weights_float = edge_weights.astype(jnp.float32)
    degree = jnp.sum(weights_float, axis=(1, 3)).reshape(sensor_rows)
    reduced = lax.psum_scatter(fit_part, ("channel", "tm"), scatter_dimension=0, tiled=True)
    whole_rows = lax.all_gather(sensor_factor, "sensor", axis=0, tiled=True)
    pulled = pulled_rows(whole_rows, neighbour_ids, weights_float, block).reshape(
        sensor_rows, rank_one
    )
    graph_all = lap_weight * (degree[:, None] * sensor_factor - pulled)
    graph_share = lax.dynamic_slice_in_dim(graph_all, share_index * share, share, 0)
    sensor_grad = reduced + graph_share
    core_grad = lax.psum(core_part, ("sensor", "channel", "tm"))
    channel_grad = lax.psum(chan_part, ("sensor", "tm"))
    time_grad = lax.psum(time_part, ("sensor", "channel"))
    return (core_grad, sensor_grad, channel_grad, time_grad)


def solution(mesh):
    return jax.shard_map(
        on_device,
        mesh=mesh,
        in_specs=(
            P("sensor", "tm", "channel"),
            P(),
            P("sensor", None),
            P("channel", None),
            P("tm", None),
            P("sensor", None),
            P("sensor", None, None, None),
        ),
        out_specs=(P(), P(("sensor", "channel", "tm"), None), P("channel", None), P("tm", None)),
        check_vma=False,
    )
```

profile of v0, /device:TPU:0, one launch (start us, length us, event | category | flops | bytes accessed | tf_op | source)
XLA Modules:
  0.0 556.5 jit_solution(13374377818562630704)
XLA Ops:
  8.0 0.0 reduce-scatter.4.cloned.1.call-start
  8.1 24.9 %copy.27 = f32[768,64,128]{0,2,1:T(8,128)} copy(f32[768,64,128]{2,1,0:T(8,128)} %param.7) | data formatting | bytes 50331648 | tf_op args[0]
  33.0 1.8 fusion.32
  34.8 1.8 fusion.5
  36.7 26.3 %bitcast_subtract_fusion = f32[768,8192]{0,1:T(8,128)} fusion(f32[768,64,128]{0,2,1:T(8,128)} %copy.27, f32[768,64]{0,1:T(8,128)S(1)} %copy-done.3, f32[8,8,64,128]{3,2,1,0:T(8,128)S(1)} %bitcast.77), kind=kOutput, calls=%fused_computation.1 | convolution fusion | flops 4838129664 | bytes 52625408 | tf_op jit(solution)/shard_map/dot_general | solution.py:32
  63.0 20.9 %fusion.14 = f32[768,64]{0,1:T(8,128)S(1)} fusion(f32[768,8192]{0,1:T(8,128)} %bitcast_subtract_fusion, f32[8,8,64,128]{3,2,1,0:T(8,128)S(1)} %bitcast.78), kind=kOutput, calls=%fused_computation.18 | convolution fusion | flops 4831887360 | bytes 27459584 | tf_op jit(solution)/shard_map/dot_general | solution.py:36
  83.8 0.9 copy.34
  84.8 0.0 reduce-scatter.4.cloned.1.call-update
  84.8 0.0 all-gather.2.cloned.1.call-start
  84.8 0.5 all-gather.2.cloned.1.call-update
  85.4 0.0 all-reduce.2.cloned.1.call-start
  85.4 27.7 %convolution_bitcast_fusion = f32[8,8,64,128]{3,1,2,0:T(8,128)S(1)} fusion(f32[768,8192]{0,1:T(8,128)} %bitcast_subtract_fusion, f32[768,64]{0,1:T(8,128)S(1)} %copy-done.4), kind=kOutput, calls=%fused_computation.12 | convolution fusion | flops 4831838208 | bytes 27459584 | tf_op jit(solution)/shard_map/dot_general | solution.py:35
  113.1 0.4 copy.39
  113.5 1.9 fusion.28
  115.4 2.2 convolution_multiply_fusion
  117.6 0.0 all-reduce.2.cloned.1.call-update
  117.6 5.2 fusion.20
  122.9 1.9 fusion.26
  124.8 0.1 copy.28
  124.9 0.1 reshape.31
  125.0 1.6 convert_reduce_fusion
  126.6 129.7 %psum.22 = f32[128,64]{0,1:T(8,128)} all-reduce(f32[128,64]{0,1:T(8,128)S(1)} %fusion.20), channel_id=1, replica_groups=mesh['sensor'=16,'channel'=4,'tm'=2] {'sensor','tm'}, use_global_device_ids=true, to_apply=%region_3.0 | all-reduce | flops 8192 | bytes 65536 | tf_op jit(solution)/shard_map/psum | solution.py:65
  256.3 3.0 fusion.23
  259.3 276.5 %psum.23 = f32[64,32]{0,1:T(8,128)} all-reduce(f32[64,32]{0,1:T(8,128)S(1)} %fusion.23), channel_id=1, replica_groups=mesh['sensor'=16,'channel'=4,'tm'=2] {'sensor','channel'}, use_global_device_ids=true, to_apply=%region_4.0 | all-reduce | flops 2048 | bytes 16384 | tf_op jit(solution)/shard_map/psum | solution.py:66
  535.8 0.1 dynamic-slice
  535.9 0.9 copy.35
  536.8 0.0 all-gather.2.cloned.1.call-done
  536.8 4.0 copy_bitcast_fusion
  540.8 2.6 gather_fusion
  543.4 1.8 fusion.11
  545.2 1.6 fusion.25
  546.8 2.3 copy.54
  (21 shorter events, 0.1 us)
Async XLA Ops:
  8.0 25.0 %copy-start = (f32[64,64,32]{1,2,0:T(8,128)S(1)}, f32[64,64,32]{1,2,0:T(8,128)}, u32[]{:S(2)}) copy-start(f32[64,64,32]{1,2,0:T(8,128)} %param.8) | copy-start | bytes 1572868
  8.0 24.9 %copy-start.6 = (f32[64,32]{0,1:T(8,128)S(1)}, f32[64,32]{0,1:T(8,128)}, u32[]{:S(2)}) copy-start(f32[64,32]{0,1:T(8,128)} %param.11) | copy-start | bytes 24580
  8.0 527.9 %reduce-scatter.4.cloned.1.call-start = ((), (), s32[]{:S(2)}) async-start(), calls=%async_computation.3 | async-start | bytes 442368
  33.0 1.8 copy-start.5
  34.8 1.9 copy-start.1
  34.8 1.9 copy-start.3
  63.0 22.5 %copy-start.4 = (f32[768,64]{0,1:T(8,128)S(1)}, f32[768,64]{0,1:T(8,128)}, u32[]{:S(2)}) copy-start(f32[768,64]{0,1:T(8,128)} %param.9) | copy-start | bytes 589828
  84.8 452.0 %all-gather.2.cloned.1.call-start = ((), (), s32[]{:S(2)}) async-start(), calls=%async_computation.2 | async-start | bytes 3342336 | tf_op jit(solution)/shard_map/all_gather | solution.py:57
  85.4 461.4 %all-reduce.2.cloned.1.call-start = ((), (), s32[]{:S(2)}) async-start(), calls=%async_computation.1 | async-start | bytes 2097152 | tf_op jit(solution)/shard_map/psum | solution.py:64
  122.9 1.9 copy-start.7
  540.8 2.6 copy-start.2
Sparse Core Ops, SparseCore 0:
  84.9 73.7 reduce-scatter.3
  164.1 146.2 all-reduce.1
Sparse Core Ops, SparseCore 1:
  87.0 38.2 all-gather.1
where the time goes:
time: 557 us; the launch traced here: 556 us
  blocking collectives  406 us (73%)
  matrix products  94.5 us (17%)
  local copies, waits for them, and re-layouts  36.2 us (6%)
  between operations  15.7 us (3%)
    psum x1, blocking collectives, on_device(): time_grad = lax.psum(time_part, ('sensor', 'channel'))  277 us
    psum x1, blocking collectives, on_device(): channel_grad = lax.psum(chan_part, ('sensor', 'tm'))  130 us
    unnamed x21, local copies, waits for them, and re-layouts  29.4 us
    dot_general x1, matrix products, on_device(): folded = jnp.dot(sensor_factor.T, residual, precision=highest)  27.7 us
    dot_general x1, matrix products, on_device(): jnp.dot(sensor_factor, flat_core, precision=highest)  26.3 us
    dot_general x1, matrix products, on_device(): jnp.dot(residual, flat_core.T, precision=highest)  20.9 us
  transfers between devices with their start and end apart: 3, of which 0 were waited for; matrix products, arithmetic and copies ran while one was open for 10% of the time, Pallas kernels for 0%

commit v1 on v0

--- a/solution.py
+++ b/solution.py
@@ -63,7 +63,7 @@
     sensor_grad = reduced + graph_share
     core_grad = lax.psum(core_part, ("sensor", "channel", "tm"))
     channel_grad = lax.psum(chan_part, ("sensor", "tm"))
-    time_grad = lax.psum(time_part, ("sensor", "channel"))
+    time_grad = lax.psum(lax.psum(time_part, "channel"), "sensor")
     return (core_grad, sensor_grad, channel_grad, time_grad)
 
 

time: 557 us -> 351 us (0.63)
  blocking collectives: 406 us -> 200 us
    psum x1 -> x2, blocking collectives: 277 us -> 69.8 us  [on_device(): time_grad = lax.psum(lax.psum(time_part, 'channel'), 'sensor')]
  transfers between devices with their start and end apart: 3 -> 3, of which waited for: 0 -> 0; matrix products, arithmetic and copies ran while one was open for 10% -> 16% of each run, Pallas kernels for 0% -> 0%
where the time goes in v1:
time: 351 us; the launch traced here: 350 us
  blocking collectives  200 us (57%)
  matrix products  94.5 us (27%)
  local copies, waits for them, and re-layouts  36.2 us (10%)
  between operations  15.7 us (4%)
    psum x1, blocking collectives, on_device(): channel_grad = lax.psum(chan_part, ('sensor', 'tm'))  130 us
    psum x2, blocking collectives, on_device(): time_grad = lax.psum(lax.psum(time_part, 'channel'), 'sensor')  69.8 us
    unnamed x21, local copies, waits for them, and re-layouts  29.3 us
    dot_general x1, matrix products, on_device(): folded = jnp.dot(sensor_factor.T, residual, precision=highest)  27.7 us
    dot_general x1, matrix products, on_device(): jnp.dot(sensor_factor, flat_core, precision=highest)  26.3 us
    dot_general x1, matrix products, on_device(): jnp.dot(residual, flat_core.T, precision=highest)  20.9 us
  transfers between devices with their start and end apart: 3, of which 0 were waited for; matrix products, arithmetic and copies ran while one was open for 16% of the time, Pallas kernels for 0%

profile of v1, /device:TPU:0, one launch (start us, length us, event | category | flops | bytes accessed | tf_op | source)
XLA Modules:
  0.0 349.8 jit_solution(13775507985205720048)
XLA Ops:
  8.0 0.0 reduce-scatter.4.cloned.1.call-start
  8.1 24.9 %copy.27 = f32[768,64,128]{0,2,1:T(8,128)} copy(f32[768,64,128]{2,1,0:T(8,128)} %param.7) | data formatting | bytes 50331648 | tf_op args[0]
  33.0 1.8 fusion.32
  34.8 1.8 fusion.5
  36.7 26.3 %bitcast_subtract_fusion = f32[768,8192]{0,1:T(8,128)} fusion(f32[768,64,128]{0,2,1:T(8,128)} %copy.27, f32[768,64]{0,1:T(8,128)S(1)} %copy-done.3, f32[8,8,64,128]{3,2,1,0:T(8,128)S(1)} %bitcast.77), kind=kOutput, calls=%fused_computation.1 | convolution fusion | flops 4838129664 | bytes 52625408 | tf_op jit(solution)/shard_map/dot_general | solution.py:32
  63.0 20.9 %fusion.14 = f32[768,64]{0,1:T(8,128)S(1)} fusion(f32[768,8192]{0,1:T(8,128)} %bitcast_subtract_fusion, f32[8,8,64,128]{3,2,1,0:T(8,128)S(1)} %bitcast.78), kind=kOutput, calls=%fused_computation.18 | convolution fusion | flops 4831887360 | bytes 27459584 | tf_op jit(solution)/shard_map/dot_general | solution.py:36
  83.8 0.9 copy.34
  84.8 0.0 reduce-scatter.4.cloned.1.call-update
  84.8 0.0 all-gather.2.cloned.1.call-start
  84.8 0.5 all-gather.2.cloned.1.call-update
  85.4 0.0 all-reduce.2.cloned.1.call-start
  85.4 27.7 %convolution_bitcast_fusion = f32[8,8,64,128]{3,1,2,0:T(8,128)S(1)} fusion(f32[768,8192]{0,1:T(8,128)} %bitcast_subtract_fusion, f32[768,64]{0,1:T(8,128)S(1)} %copy-done.4), kind=kOutput, calls=%fused_computation.12 | convolution fusion | flops 4831838208 | bytes 27459584 | tf_op jit(solution)/shard_map/dot_general | solution.py:35
  113.1 0.4 copy.39
  113.5 1.9 fusion.28
  115.4 2.2 convolution_multiply_fusion
  117.6 5.2 %fusion.20 = f32[128,64]{0,1:T(8,128)S(1)} fusion(f32[64,64,128]{2,1,0:T(8,128)S(1)} %bitcast.75, f32[64,64,64]{2,0,1:T(8,128)} %copy-done.1), kind=kOutput, calls=%fused_computation.20 | convolution fusion | flops 402661376 | bytes 3178496 | tf_op jit(solution)/shard_map/rkj,rks->js/dot_general | solution.py:44
  122.9 2.0 fusion.26
  124.8 0.1 copy.28
  124.9 0.1 reshape.31
  125.0 1.6 convert_reduce_fusion
  126.6 129.7 %psum.29 = f32[128,64]{0,1:T(8,128)} all-reduce(f32[128,64]{0,1:T(8,128)S(1)} %fusion.20), channel_id=1, replica_groups=mesh['sensor'=16,'channel'=4,'tm'=2] {'sensor','tm'}, use_global_device_ids=true, to_apply=%region_3.0 | all-reduce | flops 8192 | bytes 65536 | tf_op jit(solution)/shard_map/psum | solution.py:65
  256.3 3.0 fusion.23
  259.3 16.9 %psum.30 = f32[64,32]{0,1:T(8,128)S(1)} all-reduce(f32[64,32]{0,1:T(8,128)S(1)} %fusion.23), channel_id=1, replica_groups=mesh['sensor'=16,'channel'=4,'tm'=2] {'channel'}, use_global_device_ids=true, to_apply=%region_4.0 | all-reduce | flops 2048 | bytes 16384 | tf_op jit(solution)/shard_map/psum | solution.py:66
  276.2 52.9 %psum.31 = f32[64,32]{0,1:T(8,128)} all-reduce(f32[64,32]{0,1:T(8,128)S(1)} %psum.30), channel_id=1, replica_groups=mesh['sensor'=16,'channel'=4,'tm'=2] {'sensor'}, use_global_device_ids=true, to_apply=%region_5.0 | all-reduce | flops 2048 | bytes 16384 | tf_op jit(solution)/shard_map/psum | solution.py:66
  329.1 0.1 dynamic-slice
  329.2 0.9 copy.35
  330.1 0.0 all-gather.2.cloned.1.call-done
  330.1 4.0 %copy_bitcast_fusion = f32[96,128,64]{1,2,0:T(8,128)} fusion(f32[12288,64]{0,1:T(8,128)} %all-gather.2.cloned.1.call-done), kind=kLoop, calls=%fused_computation.2 | loop fusion | bytes 6291456 | tf_op jit(solution)/shard_map/reshape | solution.py:12
  334.1 2.6 gather_fusion
  336.7 1.8 fusion.11
  338.5 1.6 fusion.25
  340.1 2.3 copy.54
  (22 shorter events, 0.1 us)
Async XLA Ops:
  8.0 24.9 %copy-start = (f32[64,64,32]{1,2,0:T(8,128)S(1)}, f32[64,64,32]{1,2,0:T(8,128)}, u32[]{:S(2)}) copy-start(f32[64,64,32]{1,2,0:T(8,128)} %param.8) | copy-start | bytes 1572868
  8.0 24.9 %copy-start.6 = (f32[64,32]{0,1:T(8,128)S(1)}, f32[64,32]{0,1:T(8,128)}, u32[]{:S(2)}) copy-start(f32[64,32]{0,1:T(8,128)} %param.11) | copy-start | bytes 24580
  8.0 321.2 %reduce-scatter.4.cloned.1.call-start = ((), (), s32[]{:S(2)}) async-start(), calls=%async_computation.3 | async-start | bytes 442368
  32.9 1.9 copy-start.5
  34.8 1.9 copy-start.1
  34.8 1.9 copy-start.3
  63.0 22.5 %copy-start.4 = (f32[768,64]{0,1:T(8,128)S(1)}, f32[768,64]{0,1:T(8,128)}, u32[]{:S(2)}) copy-start(f32[768,64]{0,1:T(8,128)} %param.9) | copy-start | bytes 589828
  84.8 245.3 %all-gather.2.cloned.1.call-start = ((), (), s32[]{:S(2)}) async-start(), calls=%async_computation.2 | async-start | bytes 3342336 | tf_op jit(solution)/shard_map/all_gather | solution.py:57
  85.4 254.7 %all-reduce.2.cloned.1.call-start = ((), (), s32[]{:S(2)}) async-start(), calls=%async_computation.1 | async-start | bytes 2097152 | tf_op jit(solution)/shard_map/psum | solution.py:64
  122.8 2.0 copy-start.7
  334.1 2.6 copy-start.2
Sparse Core Ops, SparseCore 0:
  84.9 73.8 reduce-scatter.3
  164.1 146.0 all-reduce.1
Sparse Core Ops, SparseCore 1:
  87.0 38.2 all-gather.1
